TPU v7x, 32 devices: a whole 2x2x4 slice. The times are simulated.
32 devices in a mesh: survey: 2 (over y), gz: 4 (over z), gy: 2 (over x), pat: 2 (over core).
Axes of the slice: x: 2, y: 2, z: 4, core: 2. Of those that a mesh axis runs over, the one named last changes fastest.
Arguments:
- conductivity: float32 [32, 256, 512], P(('survey', 'gz'), 'gy'), parts along dimension 0, may hold values from 0.3 to 3
- receivers: int32 [4, 3, 64], P(('survey', 'pat')), parts along dimension 0, may hold values from 0 to 511, as said below
- observed: float32 [4, 64], P(('survey', 'pat')), parts along dimension 0, may hold values from -6 to 6
- potential: float32 [2, 32, 256, 512], P('pat', ('survey', 'gz'), 'gy'), parts along dimension 1, may hold values from -6 to 6
- adjoint_prev: float32 [2, 32, 256, 512], P('pat', ('survey', 'gz'), 'gy'), parts along dimension 1, may hold values from -0.046875 to 0.046875
Outputs:
- adjoint: float32 [2, 32, 256, 512], P('pat', ('survey', 'gz'), 'gy'), parts along dimension 1
- gradient: float32 [32, 256, 512], P(('survey', 'gz'), 'gy'), parts along dimension 0
There are 2 independent parts, one for each index of `survey`. A program takes and returns all parts, laid end to end along the dimension named above; each array names one. Nothing has to cross between parts.
Inputs may be any that keep to these rules, and one draw needn't show every extreme that they name: receivers[p, 0, r], receivers[p, 1, r] and receivers[p, 2, r] are a z cell below 16, a y cell below 256 and an x cell below 512; several receivers may share a cell.
All inputs are finite; a program needn't handle non-finite values.
Results may differ from a plain program's by a relative error of at most 0.0003.
Values sent between devices are 32-bit elements; how exact they have to be, the bound alone decides.
A program may use at most 64 MiB of HBM per device.

v0:
```python
import jax
import jax.numpy as jnp
from jax import lax
from jax.sharding import PartitionSpec as P

relax_weight = 0.8


def extended_2(cells, sides, width):
    for axis, dim in sides:
        count = lax.axis_size(axis)
        ends = count - 1
        head = lax.slice_in_dim(cells, 0, width, axis=dim)
        tail = lax.slice_in_dim(cells, cells.shape[dim] - width, cells.shape[dim], axis=dim)
        cells = jnp.concatenate(
            [
                lax.ppermute(tail, axis, [(i, (i + 1) % count) for i in range(ends)]),
                cells,
                lax.ppermute(head, axis, [((i + 1) % count, i) for i in range(ends)]),
            ],
            axis=dim,
        )
    return cells


def beside_cells(extended):
    widened = jnp.pad(extended, [(0, 0)] * (extended.ndim - 1) + [(1, 1)])
    centre = widened[..., 1:-1, 1:-1, 1:-1]
    others = [
        widened[..., 2:, 1:-1, 1:-1],
        widened[..., :-2, 1:-1, 1:-1],
        widened[..., 1:-1, 2:, 1:-1],
        widened[..., 1:-1, :-2, 1:-1],
        widened[..., 1:-1, 1:-1, 2:],
        widened[..., 1:-1, 1:-1, :-2],
    ]
    return (centre, others)


def relax(cond_ext, adjoint_ext, source):
    cond_mid, cond_near = beside_cells(cond_ext)
    adj_mid, adj_near = beside_cells(adjoint_ext)
    diagonal = jnp.zeros_like(cond_mid)
    coupled = jnp.zeros_like(adj_mid)
    for cond_side, adj_side in zip(cond_near, adj_near):
        face_coef = 0.5 * (cond_mid + cond_side)
        diagonal = diagonal + face_coef
        coupled = coupled + face_coef * adj_side
    updated = adj_mid + relax_weight * (source - diagonal * adj_mid + coupled) / diagonal
    return updated


def contribution(pot_ext, adj_ext):
    pot_mid, pot_near = beside_cells(pot_ext)
    adj_mid, adj_near = beside_cells(adj_ext)
    summed = jnp.zeros_like(adj_mid)
    for pot_side, adj_side in zip(pot_near, adj_near):
        summed = summed + (pot_mid - pot_side) * (adj_mid - adj_side)
    return -0.5 * jnp.sum(summed, axis=0)


def receiver_source(field, receivers, observed, z_start, y_start):
    z_count = field.shape[1]
    y_count = field.shape[2]
    z_local = receivers[:, 0, :] - z_start
    y_local = receivers[:, 1, :] - y_start
    x_local = receivers[:, 2, :]
    inside = (z_local >= 0) & (z_local < z_count) & (y_local >= 0) & (y_local < y_count)
    z_local = jnp.clip(z_local, 0, z_count - 1)
    y_local = jnp.clip(y_local, 0, y_count - 1)
    pattern_ids = jnp.broadcast_to(
        jnp.arange(field.shape[0], dtype=jnp.int32)[:, None], z_local.shape
    )
    values = jnp.where(
        inside, field[pattern_ids, z_local, y_local, x_local] - observed, jnp.zeros_like(observed)
    )
    return jnp.zeros_like(field).at[pattern_ids, z_local, y_local, x_local].add(values)


def local(conductivity, receivers, observed, potential, adjoint_prev):
    pattern_count = potential.shape[0]
    z_cells = conductivity.shape[0]
    y_cells = conductivity.shape[1]
    z_first = lax.axis_index("gz") * z_cells
    y_first = lax.axis_index("gy") * y_cells
    stacked = jnp.concatenate([conductivity[None], adjoint_prev], axis=0)
    extended = extended_2(stacked, (("gz", 1), ("gy", 2)), 1)
    cond_ext = extended[0]
    source = receiver_source(potential, receivers, observed, z_first, y_first)
    adjoint = relax(cond_ext, extended[1:], source)
    rimmed = extended_2(adjoint, (("gz", 1), ("gy", 2)), 1)
    adjoint = relax(cond_ext, rimmed, source)
    both_ext = extended_2(jnp.concatenate([potential, adjoint], axis=0), (("gz", 1), ("gy", 2)), 1)
    partial_grad = contribution(both_ext[:pattern_count], both_ext[pattern_count:])
    gradient = lax.psum(partial_grad, "pat")
    return (adjoint, gradient)


def solution(mesh):
    return jax.shard_map(
        local,
        mesh=mesh,
        in_specs=(
            P(("survey", "gz"), "gy", None),
            P(("survey", "pat"), None, None),
            P(("survey", "pat"), None),
            P("pat", ("survey", "gz"), "gy", None),
            P("pat", ("survey", "gz"), "gy", None),
        ),
        out_specs=(P("pat", ("survey", "gz"), "gy", None), P(("survey", "gz"), "gy", None)),
        check_vma=False,
    )
```

profile of v0, /device:TPU:0, one launch (start us, length us, event | category | flops | bytes accessed | tf_op | source)
XLA Modules:
  0.0 133.2 jit_solution(9145302090978864290)
XLA Ops:
  7.2 2.4 %pad_maximum_fusion.37 = (f32[2,1,128,512]{3,2,1,0:T(8,128)}, f32[2,1,128,512]{3,2,1,0:T(8,128)}) fusion(f32[1,4,128,512]{3,2,1,0:T(8,128)} %param.9, f32[1,4,128,512]{3,2,1,0:T(8,128)} %bitcast.63), kind=kLoop, calls=%fused_computation.126 | loop fusion | flops 262144 | bytes 3145728 | tf_op jit(solution)/shard_map/slice | solution.py:14
  9.6 5.9 %collective-permute-start = (f32[2,1,128,512]{3,2,1,0:T(8,128)}, f32[2,1,128,512]{3,2,1,0:T(8,128)}, u32[]{:S(2)}, u32[]{:S(2)}) collective-permute-start(f32[2,1,128,512]{3,2,1,0:T(8,128)} %get-tuple-element.12), channel_id=1, source_target_pairs={{0,4},{4,8},{8,12},{1,5},{5,9},{9,13},{2,6},{6,10},{10,14},{3,7},{... | collective-permute-start | bytes 1572872 | tf_op jit(solution)/shard_map/ppermute | solution.py:17
  15.5 1.3 collective-permute-start.1
  16.9 1.0 gather_fusion
  17.9 8.3 %collective-permute-done = f32[2,1,128,512]{3,2,1,0:T(8,128)} collective-permute-done((f32[2,1,128,512]{3,2,1,0:T(8,128)}, f32[2,1,128,512]{3,2,1,0:T(8,128)}, u32[]{:S(2)}, u32[]{:S(2)}) %collective-permute-start) | collective-permute-done | bytes 524320 | tf_op jit(solution)/shard_map/ppermute | solution.py:17
  26.2 4.9 %collective-permute-done.1 = f32[2,1,128,512]{3,2,1,0:T(8,128)} collective-permute-done((f32[2,1,128,512]{3,2,1,0:T(8,128)}, f32[2,1,128,512]{3,2,1,0:T(8,128)}, u32[]{:S(2)}, u32[]{:S(2)}) %collective-permute-start.1) | collective-permute-done | bytes 524320 | tf_op jit(solution)/shard_map/ppermute | solution.py:19
  31.1 0.8 pad_maximum_fusion.45
  32.0 3.4 %collective-permute-start.2 = (f32[2,6,1,512]{3,2,1,0:T(1,128)S(1)}, f32[2,6,1,512]{3,2,1,0:T(1,128)S(1)}, u32[]{:S(2)}, u32[]{:S(2)}) collective-permute-start(f32[2,6,1,512]{3,2,1,0:T(1,128)S(1)} %get-tuple-element.8), channel_id=1, source_target_pairs={{0,2},{1,3},{4,6},{5,7},{8,10},{9,11},{12,14},{13,15},{16,18},{17,... | collective-permute-start | bytes 73736 | tf_op jit(solution)/shard_map/ppermute | solution.py:17
  35.4 1.3 collective-permute-start.3
  36.7 1.1 broadcast.273
  37.8 9.4 %scatter_fusion = f32[4,128,512]{2,1,0:T(8,128)} fusion(f32[4,128,512]{2,1,0:T(8,128)} %broadcast.273, s32[64]{0:T(128)S(1)} %get-tuple-element.19, f32[64]{0:T(128)S(1)} %fusion.63), kind=kCustom, calls=%fused_computation.1 | custom fusion | flops 64 | bytes 1536 | tf_op jit(solution)/shard_map/scatter-add | solution.py:77
  47.2 1.7 %pad_maximum_fusion = f32[2,6,130,512]{3,2,1,0:T(8,128)S(1)} fusion(f32[2,6,1,512]{3,2,1,0:T(1,128)S(1)} %collective-permute-done.3, f32[2,1,128,512]{3,2,1,0:T(8,128)} %collective-permute-done.1, f32[1,4,128,512]{3,2,1,0:T(8,128)S(1)} %copy-done.2, f32[1,4,128,512]{3,2,1,0:T(8,128)S(1)} %bitcast.65, f32[2,1,128,512]{3,2,1,0:T(8,128)} %collective-permute-done, ...), kind=kLoop, calls=%fused_computation.2 | loop fusion | flops 3993600 | bytes 6389760 | tf_op jit(solution)/shard_map/concatenate | solution.py:15
  49.2 0.9 copy-done.4
  50.1 4.7 %fusion.11 = f32[1,4,128,512]{3,2,1,0:T(8,128)S(1)} fusion(f32[1,4,128,512]{3,2,1,0:T(8,128)S(1)} %copy-done.2, f32[1,6,130,512]{3,2,1,0:T(8,128)S(1)} %get-tuple-element.5, f32[2,6,1,512]{3,2,1,0:T(1,128)S(1)} %collective-permute-done.2, f32[2,1,128,512]{3,2,1,0:T(8,128)} %collective-permute-done.1, f32[2,1,128,512]{3,2,1,0:T(8,128)} %collective-permute-done, ...), kind=kLoop, calls=%fused_computation.30 | loop fusion | flops 12058624 | bytes 13877248 | tf_op jit(solution)/shard_map/add | solution.py:49
  54.8 2.7 %collective-permute-start.5 = (f32[1,1,128,512]{3,2,1,0:T(8,128)S(1)}, f32[1,1,128,512]{3,2,1,0:T(8,128)S(1)}, u32[]{:S(2)}, u32[]{:S(2)}) collective-permute-start(f32[1,1,128,512]{3,2,1,0:T(8,128)S(1)} %get-tuple-element.16), channel_id=1, source_target_pairs={{0,4},{4,8},{8,12},{1,5},{5,9},{9,13},{2,6},{6,10},{10,14},{3,7},{... | collective-permute-start | bytes 786440 | tf_op jit(solution)/shard_map/ppermute | solution.py:17
  57.5 1.3 collective-permute-start.4
  58.8 2.8 %collective-permute-done.5 = f32[1,1,128,512]{3,2,1,0:T(8,128)S(1)} collective-permute-done((f32[1,1,128,512]{3,2,1,0:T(8,128)S(1)}, f32[1,1,128,512]{3,2,1,0:T(8,128)S(1)}, u32[]{:S(2)}, u32[]{:S(2)}) %collective-permute-start.5) | collective-permute-done | bytes 262176 | tf_op jit(solution)/shard_map/ppermute | solution.py:17
  61.6 4.2 %collective-permute-done.4 = f32[1,1,128,512]{3,2,1,0:T(8,128)S(1)} collective-permute-done((f32[1,1,128,512]{3,2,1,0:T(8,128)S(1)}, f32[1,1,128,512]{3,2,1,0:T(8,128)S(1)}, u32[]{:S(2)}, u32[]{:S(2)}) %collective-permute-start.4) | collective-permute-done | bytes 262176 | tf_op jit(solution)/shard_map/ppermute | solution.py:19
  65.8 4.6 %collective-permute-start.7 = (f32[1,6,1,512]{3,2,1,0:T(1,128)S(1)}, f32[1,6,1,512]{3,2,1,0:T(1,128)S(1)}, u32[]{:S(2)}, u32[]{:S(2)}) collective-permute-start(f32[1,6,1,512]{3,2,1,0:T(1,128)S(1)} %get-tuple-element.14), channel_id=1, source_target_pairs={{0,2},{1,3},{4,6},{5,7},{8,10},{9,11},{12,14},{13,15},{16,18},{17,... | collective-permute-start | bytes 36872 | tf_op jit(solution)/shard_map/ppermute | solution.py:17
  70.3 1.3 collective-permute-start.6
  71.7 4.2 %collective-permute-done.6 = f32[1,6,1,512]{3,2,1,0:T(1,128)S(1)} collective-permute-done((f32[1,6,1,512]{3,2,1,0:T(1,128)S(1)}, f32[1,6,1,512]{3,2,1,0:T(1,128)S(1)}, u32[]{:S(2)}, u32[]{:S(2)}) %collective-permute-start.6) | collective-permute-done | bytes 12320 | tf_op jit(solution)/shard_map/ppermute | solution.py:19
  76.7 3.4 %fusion.38 = f32[1,4,128,512]{3,2,1,0:T(8,128)S(1)} fusion(f32[1,4,128,512]{3,2,1,0:T(8,128)S(1)} %fusion.11, f32[1,6,130,514]{3,2,1,0:T(8,128)S(1)} %select_maximum_fusion, f32[1,6,1,512]{3,2,1,0:T(1,128)S(1)} %collective-permute-done.7, f32[1,1,128,512]{3,2,1,0:T(8,128)S(1)} %collective-permute-done.4, f32[1,1,128,512]{3,2,1,0:T(8,128)S(1)} %collective-permute-done.5, ...), kind=kLoop, calls=%fused_computation.74 | loop fusion | flops 11010048 | bytes 12705792 | tf_op jit(solution)/shard_map/add | solution.py:49
  80.2 3.6 %collective-permute-start.9 = (f32[2,1,128,512]{3,2,1,0:T(8,128)S(1)}, f32[2,1,128,512]{3,2,1,0:T(8,128)S(1)}, u32[]{:S(2)}, u32[]{:S(2)}) collective-permute-start(f32[2,1,128,512]{3,2,1,0:T(8,128)S(1)} %get-tuple-element.10), channel_id=1, source_target_pairs={{0,4},{4,8},{8,12},{1,5},{5,9},{9,13},{2,6},{6,10},{10,14},{3,7},{... | collective-permute-start | bytes 1572872 | tf_op jit(solution)/shard_map/ppermute | solution.py:17
  83.8 1.3 collective-permute-start.8
  85.1 5.3 %collective-permute-done.9 = f32[2,1,128,512]{3,2,1,0:T(8,128)S(1)} collective-permute-done((f32[2,1,128,512]{3,2,1,0:T(8,128)S(1)}, f32[2,1,128,512]{3,2,1,0:T(8,128)S(1)}, u32[]{:S(2)}, u32[]{:S(2)}) %collective-permute-start.9) | collective-permute-done | bytes 524320 | tf_op jit(solution)/shard_map/ppermute | solution.py:17
  90.4 4.4 %collective-permute-done.8 = f32[2,1,128,512]{3,2,1,0:T(8,128)S(1)} collective-permute-done((f32[2,1,128,512]{3,2,1,0:T(8,128)S(1)}, f32[2,1,128,512]{3,2,1,0:T(8,128)S(1)}, u32[]{:S(2)}, u32[]{:S(2)}) %collective-permute-start.8) | collective-permute-done | bytes 524320 | tf_op jit(solution)/shard_map/ppermute | solution.py:19
  94.9 1.6 %collective-permute-start.11 = (f32[2,6,1,512]{3,2,1,0:T(1,128)S(1)}, f32[2,6,1,512]{3,2,1,0:T(1,128)S(1)}, u32[]{:S(2)}, u32[]{:S(2)}) collective-permute-start(f32[2,6,1,512]{3,2,1,0:T(1,128)S(1)} %get-tuple-element.6), channel_id=1, source_target_pairs={{0,2},{1,3},{4,6},{5,7},{8,10},{9,11},{12,14},{13,15},{16,18},{17,... | collective-permute-start | bytes 73736 | tf_op jit(solution)/shard_map/ppermute | solution.py:17
  96.6 1.3 collective-permute-start.10
  98.1 4.2 %collective-permute-done.10 = f32[2,6,1,512]{3,2,1,0:T(1,128)S(1)} collective-permute-done((f32[2,6,1,512]{3,2,1,0:T(1,128)S(1)}, f32[2,6,1,512]{3,2,1,0:T(1,128)S(1)}, u32[]{:S(2)}, u32[]{:S(2)}) %collective-permute-start.10) | collective-permute-done | bytes 24608 | tf_op jit(solution)/shard_map/ppermute | solution.py:19
  103.1 4.3 %fusion.18 = f32[4,128,512]{2,1,0:T(8,128)} fusion(f32[1,4,128,512]{3,2,1,0:T(8,128)S(1)} %copy-done.1, f32[1,6,130,512]{3,2,1,0:T(8,128)S(1)} %get-tuple-element.3, f32[1,4,128,512]{3,2,1,0:T(8,128)S(1)} %fusion.38, f32[1,6,130,512]{3,2,1,0:T(8,128)S(1)} %get-tuple-element.2, f32[2,6,1,512]{3,2,1,0:T(1,128)S(1)} %collective-permute-done.11, ...), kind=kLoop, calls=%fused_computation.37 | loop fusion | flops 12582912 | bytes 7438336 | tf_op jit(solution)/shard_map/mul | solution.py:59
  107.4 16.7 %all-reduce.7.cloned.1.call-done = f32[4,128,512]{2,1,0:T(8,128)} async-done(((f32[4,128,512]{2,1,0:T(8,128)}), f32[4,128,512]{2,1,0:T(8,128)}) %all-reduce.7.cloned.1.call-update) | async-done | bytes 1048592 | tf_op jit(solution)/shard_map/psum | solution.py:95
  124.1 2.3 %copy.9 = f32[4,128,512]{2,1,0:T(8,128)} copy(f32[4,128,512]{2,1,0:T(8,128)} %all-reduce.7.cloned.1.call-done) | data formatting | bytes 2097152
  (32 shorter events, 2.5 us)
Async XLA Ops:
  7.2 23.9 %copy-start.2 = (f32[1,4,128,512]{3,2,1,0:T(8,128)S(1)}, f32[1,4,128,512]{3,2,1,0:T(8,128)}, u32[]{:S(2)}) copy-start(f32[1,4,128,512]{3,2,1,0:T(8,128)} %param.9) | copy-start | bytes 3145732
  7.2 23.9 %copy-start.3 = (f32[4,128,512]{2,1,0:T(8,128)S(1)}, f32[4,128,512]{2,1,0:T(8,128)}, u32[]{:S(2)}) copy-start(f32[4,128,512]{2,1,0:T(8,128)} %param.5) | copy-start | bytes 3145732
  7.2 9.6 %copy-start.5 = (s32[1,3,64]{2,0,1:T(1,128)S(1)}, s32[1,3,64]{2,0,1:T(1,128)}, u32[]{:S(2)}) copy-start(s32[1,3,64]{2,0,1:T(1,128)} %param.6) | copy-start | bytes 2308
  7.2 9.7 %copy-start.1 = (f32[1,4,128,512]{3,2,1,0:T(8,128)S(1)}, f32[1,4,128,512]{3,2,1,0:T(8,128)}, u32[]{:S(2)}) copy-start(f32[1,4,128,512]{3,2,1,0:T(8,128)} %param.8) | copy-start | bytes 3145732
  7.2 116.9 %all-reduce.7.cloned.1.call-start = ((), (), s32[]{:S(2)}) async-start(), calls=%async_computation | async-start | bytes 2097152 | tf_op jit(solution)/shard_map/psum | solution.py:95
  9.6 27.0 %copy-start.6 = (f32[1,64]{1,0:T(1,128)S(1)}, f32[1,64]{1,0:T(1,128)}, u32[]{:S(2)}) copy-start(f32[1,64]{1,0:T(1,128)} %param.7) | copy-start | bytes 772
  9.6 16.6 %collective-permute-start = (f32[2,1,128,512]{3,2,1,0:T(8,128)}, f32[2,1,128,512]{3,2,1,0:T(8,128)}, u32[]{:S(2)}, u32[]{:S(2)}) collective-permute-start(f32[2,1,128,512]{3,2,1,0:T(8,128)} %get-tuple-element.12), channel_id=1, source_target_pairs={{0,4},{4,8},{8,12},{1,5},{5,9},{9,13},{2,6},{6,10},{10,14},{3,7},{... | collective-permute-start | bytes 1572872 | tf_op jit(solution)/shard_map/ppermute | solution.py:17
  15.5 15.6 %collective-permute-start.1 = (f32[2,1,128,512]{3,2,1,0:T(8,128)}, f32[2,1,128,512]{3,2,1,0:T(8,128)}, u32[]{:S(2)}, u32[]{:S(2)}) collective-permute-start(f32[2,1,128,512]{3,2,1,0:T(8,128)} %get-tuple-element.13), channel_id=1, source_target_pairs={{4,0},{8,4},{12,8},{5,1},{9,5},{13,9},{6,2},{10,6},{14,10},{7,3},{... | collective-permute-start | bytes 1572872 | tf_op jit(solution)/shard_map/ppermute | solution.py:19
  32.0 15.2 %collective-permute-start.2 = (f32[2,6,1,512]{3,2,1,0:T(1,128)S(1)}, f32[2,6,1,512]{3,2,1,0:T(1,128)S(1)}, u32[]{:S(2)}, u32[]{:S(2)}) collective-permute-start(f32[2,6,1,512]{3,2,1,0:T(1,128)S(1)} %get-tuple-element.8), channel_id=1, source_target_pairs={{0,2},{1,3},{4,6},{5,7},{8,10},{9,11},{12,14},{13,15},{16,18},{17,... | collective-permute-start | bytes 73736 | tf_op jit(solution)/shard_map/ppermute | solution.py:17
  35.4 11.8 %collective-permute-start.3 = (f32[2,6,1,512]{3,2,1,0:T(1,128)S(1)}, f32[2,6,1,512]{3,2,1,0:T(1,128)S(1)}, u32[]{:S(2)}, u32[]{:S(2)}) collective-permute-start(f32[2,6,1,512]{3,2,1,0:T(1,128)S(1)} %get-tuple-element.9), channel_id=1, source_target_pairs={{2,0},{3,1},{6,4},{7,5},{10,8},{11,9},{14,12},{15,13},{18,16},{19,... | collective-permute-start | bytes 73736 | tf_op jit(solution)/shard_map/ppermute | solution.py:19
  48.8 1.2 copy-start.4
  54.8 6.8 %collective-permute-start.5 = (f32[1,1,128,512]{3,2,1,0:T(8,128)S(1)}, f32[1,1,128,512]{3,2,1,0:T(8,128)S(1)}, u32[]{:S(2)}, u32[]{:S(2)}) collective-permute-start(f32[1,1,128,512]{3,2,1,0:T(8,128)S(1)} %get-tuple-element.16), channel_id=1, source_target_pairs={{0,4},{4,8},{8,12},{1,5},{5,9},{9,13},{2,6},{6,10},{10,14},{3,7},{... | collective-permute-start | bytes 786440 | tf_op jit(solution)/shard_map/ppermute | solution.py:17
  57.5 8.3 %collective-permute-start.4 = (f32[1,1,128,512]{3,2,1,0:T(8,128)S(1)}, f32[1,1,128,512]{3,2,1,0:T(8,128)S(1)}, u32[]{:S(2)}, u32[]{:S(2)}) collective-permute-start(f32[1,1,128,512]{3,2,1,0:T(8,128)S(1)} %get-tuple-element.17), channel_id=1, source_target_pairs={{4,0},{8,4},{12,8},{5,1},{9,5},{13,9},{6,2},{10,6},{14,10},{7,3},{... | collective-permute-start | bytes 786440 | tf_op jit(solution)/shard_map/ppermute | solution.py:19
  65.8 6.0 %collective-permute-start.7 = (f32[1,6,1,512]{3,2,1,0:T(1,128)S(1)}, f32[1,6,1,512]{3,2,1,0:T(1,128)S(1)}, u32[]{:S(2)}, u32[]{:S(2)}) collective-permute-start(f32[1,6,1,512]{3,2,1,0:T(1,128)S(1)} %get-tuple-element.14), channel_id=1, source_target_pairs={{0,2},{1,3},{4,6},{5,7},{8,10},{9,11},{12,14},{13,15},{16,18},{17,... | collective-permute-start | bytes 36872 | tf_op jit(solution)/shard_map/ppermute | solution.py:17
  70.3 5.6 %collective-permute-start.6 = (f32[1,6,1,512]{3,2,1,0:T(1,128)S(1)}, f32[1,6,1,512]{3,2,1,0:T(1,128)S(1)}, u32[]{:S(2)}, u32[]{:S(2)}) collective-permute-start(f32[1,6,1,512]{3,2,1,0:T(1,128)S(1)} %get-tuple-element.15), channel_id=1, source_target_pairs={{2,0},{3,1},{6,4},{7,5},{10,8},{11,9},{14,12},{15,13},{18,16},{19,... | collective-permute-start | bytes 36872 | tf_op jit(solution)/shard_map/ppermute | solution.py:19
  80.1 23.0 %copy-start = (f32[1,4,128,512]{3,2,1,0:T(8,128)}, f32[1,4,128,512]{3,2,1,0:T(8,128)S(1)}, u32[]{:S(2)}) copy-start(f32[1,4,128,512]{3,2,1,0:T(8,128)S(1)} %fusion.38) | copy-start | bytes 3145732
  80.2 10.2 %collective-permute-start.9 = (f32[2,1,128,512]{3,2,1,0:T(8,128)S(1)}, f32[2,1,128,512]{3,2,1,0:T(8,128)S(1)}, u32[]{:S(2)}, u32[]{:S(2)}) collective-permute-start(f32[2,1,128,512]{3,2,1,0:T(8,128)S(1)} %get-tuple-element.10), channel_id=1, source_target_pairs={{0,4},{4,8},{8,12},{1,5},{5,9},{9,13},{2,6},{6,10},{10,14},{3,7},{... | collective-permute-start | bytes 1572872 | tf_op jit(solution)/shard_map/ppermute | solution.py:17
  83.8 11.1 %collective-permute-start.8 = (f32[2,1,128,512]{3,2,1,0:T(8,128)S(1)}, f32[2,1,128,512]{3,2,1,0:T(8,128)S(1)}, u32[]{:S(2)}, u32[]{:S(2)}) collective-permute-start(f32[2,1,128,512]{3,2,1,0:T(8,128)S(1)} %get-tuple-element.11), channel_id=1, source_target_pairs={{4,0},{8,4},{12,8},{5,1},{9,5},{13,9},{6,2},{10,6},{14,10},{7,3},{... | collective-permute-start | bytes 1572872 | tf_op jit(solution)/shard_map/ppermute | solution.py:19
  94.9 3.2 %collective-permute-start.11 = (f32[2,6,1,512]{3,2,1,0:T(1,128)S(1)}, f32[2,6,1,512]{3,2,1,0:T(1,128)S(1)}, u32[]{:S(2)}, u32[]{:S(2)}) collective-permute-start(f32[2,6,1,512]{3,2,1,0:T(1,128)S(1)} %get-tuple-element.6), channel_id=1, source_target_pairs={{0,2},{1,3},{4,6},{5,7},{8,10},{9,11},{12,14},{13,15},{16,18},{17,... | collective-permute-start | bytes 73736 | tf_op jit(solution)/shard_map/ppermute | solution.py:17
  96.6 5.7 %collective-permute-start.10 = (f32[2,6,1,512]{3,2,1,0:T(1,128)S(1)}, f32[2,6,1,512]{3,2,1,0:T(1,128)S(1)}, u32[]{:S(2)}, u32[]{:S(2)}) collective-permute-start(f32[2,6,1,512]{3,2,1,0:T(1,128)S(1)} %get-tuple-element.7), channel_id=1, source_target_pairs={{2,0},{3,1},{6,4},{7,5},{10,8},{11,9},{14,12},{15,13},{18,16},{19,... | collective-permute-start | bytes 73736 | tf_op jit(solution)/shard_map/ppermute | solution.py:19
Sparse Core Ops, SparseCore 0:
  107.5 16.5 all-reduce.6
where the time goes:
time: 134 us; the launch traced here: 133 us
  waiting for transfers between devices  55.4 us (41%)
  starting transfers between devices  29.5 us (22%)
  other arithmetic  28 us (21%)
  between operations  14.3 us (11%)
  local copies, waits for them, and re-layouts  5.99 us (4%)
    ppermute x6, waiting for transfers between devices, extended_2(): lax.ppermute(head, axis, [((i + 1) % count, i) for i in range(ends)])  21.9 us
    ppermute x6, starting transfers between devices, extended_2(): lax.ppermute(tail, axis, [(i, (i + 1) % count) for i in range(ends)])  21.7 us
    ppermute x6, waiting for transfers between devices, extended_2(): lax.ppermute(tail, axis, [(i, (i + 1) % count) for i in range(ends)])  16.7 us
    psum x1, waiting for transfers between devices, local(): gradient = lax.psum(partial_grad, 'pat')  16.7 us
    scatter-add x1, other arithmetic, receiver_source(): jnp.zeros_like(field).at[pattern_ids, z_local, y_local, x_local].add(values)  9.4 us
    add x2, other arithmetic, relax(): adj_mid + relax_weight * (source - diagonal * adj_mid + coupled) / diagonal  8.09 us
    ppermute x6, starting transfers between devices, extended_2(): lax.ppermute(head, axis, [((i + 1) % count, i) for i in range(ends)])  7.74 us
    mul x1, other arithmetic, contribution(): return -0.5 * jnp.sum(summed, axis=0)  4.25 us
  transfers between devices with their start and end apart: 13, of which 11 were waited for; matrix products, arithmetic and copies ran while one was open for 9% of the time, Pallas kernels for 0%

commit v1 on v0

--- a/solution.py
+++ b/solution.py
@@ -92,7 +92,7 @@
     adjoint = relax(cond_ext, rimmed, source)
     both_ext = extended_2(jnp.concatenate([potential, adjoint], axis=0), (("gz", 1), ("gy", 2)), 1)
     partial_grad = contribution(both_ext[:pattern_count], both_ext[pattern_count:])
-    gradient = lax.psum(partial_grad, "pat")
+    gradient = lax.all_gather(partial_grad, axis_name="pat").sum(axis=0)
     return (adjoint, gradient)
 
 

time: 134 us -> 126 us (0.940)
  waiting for transfers between devices: 55.4 us -> 46.6 us
  other arithmetic: 28 us -> 30.9 us
  local copies, waits for them, and re-layouts: 5.99 us -> 3.73 us
    psum x1 -> x0, waiting for transfers between devices: 16.7 us -> none  [local(): gradient = lax.psum(partial_grad, 'pat')]
    all_gather x0 -> x1, waiting for transfers between devices: none -> 7.9 us  [local(): gradient = lax.all_gather(partial_grad, axis_name='pat').sum(axis=0)]
    reduce_sum x0 -> x1, other arithmetic: none -> 2.87 us  [local(): gradient = lax.all_gather(partial_grad, axis_name='pat').sum(axis=0)]
    unnamed x15 -> x14, local copies, waits for them, and re-layouts: 3.15 us -> 0.89 us
where the time goes in v1:
time: 126 us; the launch traced here: 125 us
  waiting for transfers between devices  46.6 us (37%)
  other arithmetic  30.9 us (25%)
  starting transfers between devices  29.5 us (23%)
  between operations  14.3 us (11%)
  local copies, waits for them, and re-layouts  3.73 us (3%)
    ppermute x6, waiting for transfers between devices, extended_2(): lax.ppermute(head, axis, [((i + 1) % count, i) for i in range(ends)])  21.9 us
    ppermute x6, starting transfers between devices, extended_2(): lax.ppermute(tail, axis, [(i, (i + 1) % count) for i in range(ends)])  21.7 us
    ppermute x6, waiting for transfers between devices, extended_2(): lax.ppermute(tail, axis, [(i, (i + 1) % count) for i in range(ends)])  16.7 us
    scatter-add x1, other arithmetic, receiver_source(): jnp.zeros_like(field).at[pattern_ids, z_local, y_local, x_local].add(values)  9.4 us
    add x2, other arithmetic, relax(): adj_mid + relax_weight * (source - diagonal * adj_mid + coupled) / diagonal  8.09 us
    all_gather x1, waiting for transfers between devices, local(): gradient = lax.all_gather(partial_grad, axis_name='pat').sum(axis=0)  7.9 us
    ppermute x6, starting transfers between devices, extended_2(): lax.ppermute(head, axis, [((i + 1) % count, i) for i in range(ends)])  7.74 us
    mul x1, other arithmetic, contribution(): return -0.5 * jnp.sum(summed, axis=0)  4.35 us
  transfers between devices with their start and end apart: 13, of which 11 were waited for; matrix products, arithmetic and copies ran while one was open for 9% of the time, Pallas kernels for 0%

profile of v1, /device:TPU:0, one launch (start us, length us, event | category | flops | bytes accessed | tf_op | source)
XLA Modules:
  0.0 125.1 jit_solution(14226037504741916804)
XLA Ops:
  7.2 2.4 %pad_maximum_fusion.37 = (f32[2,1,128,512]{3,2,1,0:T(8,128)}, f32[2,1,128,512]{3,2,1,0:T(8,128)}) fusion(f32[1,4,128,512]{3,2,1,0:T(8,128)} %param.9, f32[1,4,128,512]{3,2,1,0:T(8,128)} %bitcast.61), kind=kLoop, calls=%fused_computation.125 | loop fusion | flops 262144 | bytes 3145728 | tf_op jit(solution)/shard_map/slice | solution.py:14
  9.6 5.9 %collective-permute-start = (f32[2,1,128,512]{3,2,1,0:T(8,128)}, f32[2,1,128,512]{3,2,1,0:T(8,128)}, u32[]{:S(2)}, u32[]{:S(2)}) collective-permute-start(f32[2,1,128,512]{3,2,1,0:T(8,128)} %get-tuple-element.12), channel_id=1, source_target_pairs={{0,4},{4,8},{8,12},{1,5},{5,9},{9,13},{2,6},{6,10},{10,14},{3,7},{... | collective-permute-start | bytes 1572872 | tf_op jit(solution)/shard_map/ppermute | solution.py:17
  15.5 1.3 %collective-permute-start.1 = (f32[2,1,128,512]{3,2,1,0:T(8,128)}, f32[2,1,128,512]{3,2,1,0:T(8,128)}, u32[]{:S(2)}, u32[]{:S(2)}) collective-permute-start(f32[2,1,128,512]{3,2,1,0:T(8,128)} %get-tuple-element.13), channel_id=1, source_target_pairs={{4,0},{8,4},{12,8},{5,1},{9,5},{13,9},{6,2},{10,6},{14,10},{7,3},{... | collective-permute-start | bytes 1572872 | tf_op jit(solution)/shard_map/ppermute | solution.py:19
  16.9 1.0 gather_fusion
  17.9 8.3 %collective-permute-done = f32[2,1,128,512]{3,2,1,0:T(8,128)} collective-permute-done((f32[2,1,128,512]{3,2,1,0:T(8,128)}, f32[2,1,128,512]{3,2,1,0:T(8,128)}, u32[]{:S(2)}, u32[]{:S(2)}) %collective-permute-start) | collective-permute-done | bytes 524320 | tf_op jit(solution)/shard_map/ppermute | solution.py:17
  26.2 4.9 %collective-permute-done.1 = f32[2,1,128,512]{3,2,1,0:T(8,128)} collective-permute-done((f32[2,1,128,512]{3,2,1,0:T(8,128)}, f32[2,1,128,512]{3,2,1,0:T(8,128)}, u32[]{:S(2)}, u32[]{:S(2)}) %collective-permute-start.1) | collective-permute-done | bytes 524320 | tf_op jit(solution)/shard_map/ppermute | solution.py:19
  31.1 0.8 pad_maximum_fusion.45
  32.0 3.4 %collective-permute-start.2 = (f32[2,6,1,512]{3,2,1,0:T(1,128)S(1)}, f32[2,6,1,512]{3,2,1,0:T(1,128)S(1)}, u32[]{:S(2)}, u32[]{:S(2)}) collective-permute-start(f32[2,6,1,512]{3,2,1,0:T(1,128)S(1)} %get-tuple-element.8), channel_id=1, source_target_pairs={{0,2},{1,3},{4,6},{5,7},{8,10},{9,11},{12,14},{13,15},{16,18},{17,... | collective-permute-start | bytes 73736 | tf_op jit(solution)/shard_map/ppermute | solution.py:17
  35.4 1.3 %collective-permute-start.3 = (f32[2,6,1,512]{3,2,1,0:T(1,128)S(1)}, f32[2,6,1,512]{3,2,1,0:T(1,128)S(1)}, u32[]{:S(2)}, u32[]{:S(2)}) collective-permute-start(f32[2,6,1,512]{3,2,1,0:T(1,128)S(1)} %get-tuple-element.9), channel_id=1, source_target_pairs={{2,0},{3,1},{6,4},{7,5},{10,8},{11,9},{14,12},{15,13},{18,16},{19,... | collective-permute-start | bytes 73736 | tf_op jit(solution)/shard_map/ppermute | solution.py:19
  36.7 1.1 broadcast.272
  37.8 9.4 %scatter_fusion = f32[4,128,512]{2,1,0:T(8,128)} fusion(f32[4,128,512]{2,1,0:T(8,128)} %broadcast.272, s32[64]{0:T(128)S(1)} %get-tuple-element.19, f32[64]{0:T(128)S(1)} %fusion.62), kind=kCustom, calls=%fused_computation.1 | custom fusion | flops 64 | bytes 1536 | tf_op jit(solution)/shard_map/scatter-add | solution.py:77
  47.2 1.7 %pad_maximum_fusion = f32[2,6,130,512]{3,2,1,0:T(8,128)S(1)} fusion(f32[2,6,1,512]{3,2,1,0:T(1,128)S(1)} %collective-permute-done.3, f32[2,1,128,512]{3,2,1,0:T(8,128)} %collective-permute-done.1, f32[1,4,128,512]{3,2,1,0:T(8,128)S(1)} %copy-done.2, f32[1,4,128,512]{3,2,1,0:T(8,128)S(1)} %bitcast.63, f32[2,1,128,512]{3,2,1,0:T(8,128)} %collective-permute-done, ...), kind=kLoop, calls=%fused_computation.2 | loop fusion | flops 3993600 | bytes 6389760 | tf_op jit(solution)/shard_map/concatenate | solution.py:15
  49.2 0.9 copy-done.4
  50.1 4.7 %fusion.11 = f32[1,4,128,512]{3,2,1,0:T(8,128)S(1)} fusion(f32[1,4,128,512]{3,2,1,0:T(8,128)S(1)} %copy-done.2, f32[1,6,130,512]{3,2,1,0:T(8,128)S(1)} %get-tuple-element.5, f32[2,6,1,512]{3,2,1,0:T(1,128)S(1)} %collective-permute-done.2, f32[2,1,128,512]{3,2,1,0:T(8,128)} %collective-permute-done.1, f32[2,1,128,512]{3,2,1,0:T(8,128)} %collective-permute-done, ...), kind=kLoop, calls=%fused_computation.30 | loop fusion | flops 12058624 | bytes 13877248 | tf_op jit(solution)/shard_map/add | solution.py:49
  54.8 2.7 %collective-permute-start.5 = (f32[1,1,128,512]{3,2,1,0:T(8,128)S(1)}, f32[1,1,128,512]{3,2,1,0:T(8,128)S(1)}, u32[]{:S(2)}, u32[]{:S(2)}) collective-permute-start(f32[1,1,128,512]{3,2,1,0:T(8,128)S(1)} %get-tuple-element.16), channel_id=1, source_target_pairs={{0,4},{4,8},{8,12},{1,5},{5,9},{9,13},{2,6},{6,10},{10,14},{3,7},{... | collective-permute-start | bytes 786440 | tf_op jit(solution)/shard_map/ppermute | solution.py:17
  57.5 1.3 %collective-permute-start.4 = (f32[1,1,128,512]{3,2,1,0:T(8,128)S(1)}, f32[1,1,128,512]{3,2,1,0:T(8,128)S(1)}, u32[]{:S(2)}, u32[]{:S(2)}) collective-permute-start(f32[1,1,128,512]{3,2,1,0:T(8,128)S(1)} %get-tuple-element.17), channel_id=1, source_target_pairs={{4,0},{8,4},{12,8},{5,1},{9,5},{13,9},{6,2},{10,6},{14,10},{7,3},{... | collective-permute-start | bytes 786440 | tf_op jit(solution)/shard_map/ppermute | solution.py:19
  58.8 2.8 %collective-permute-done.5 = f32[1,1,128,512]{3,2,1,0:T(8,128)S(1)} collective-permute-done((f32[1,1,128,512]{3,2,1,0:T(8,128)S(1)}, f32[1,1,128,512]{3,2,1,0:T(8,128)S(1)}, u32[]{:S(2)}, u32[]{:S(2)}) %collective-permute-start.5) | collective-permute-done | bytes 262176 | tf_op jit(solution)/shard_map/ppermute | solution.py:17
  61.6 4.2 %collective-permute-done.4 = f32[1,1,128,512]{3,2,1,0:T(8,128)S(1)} collective-permute-done((f32[1,1,128,512]{3,2,1,0:T(8,128)S(1)}, f32[1,1,128,512]{3,2,1,0:T(8,128)S(1)}, u32[]{:S(2)}, u32[]{:S(2)}) %collective-permute-start.4) | collective-permute-done | bytes 262176 | tf_op jit(solution)/shard_map/ppermute | solution.py:19
  65.8 4.6 %collective-permute-start.7 = (f32[1,6,1,512]{3,2,1,0:T(1,128)S(1)}, f32[1,6,1,512]{3,2,1,0:T(1,128)S(1)}, u32[]{:S(2)}, u32[]{:S(2)}) collective-permute-start(f32[1,6,1,512]{3,2,1,0:T(1,128)S(1)} %get-tuple-element.14), channel_id=1, source_target_pairs={{0,2},{1,3},{4,6},{5,7},{8,10},{9,11},{12,14},{13,15},{16,18},{17,... | collective-permute-start | bytes 36872 | tf_op jit(solution)/shard_map/ppermute | solution.py:17
  70.3 1.3 %collective-permute-start.6 = (f32[1,6,1,512]{3,2,1,0:T(1,128)S(1)}, f32[1,6,1,512]{3,2,1,0:T(1,128)S(1)}, u32[]{:S(2)}, u32[]{:S(2)}) collective-permute-start(f32[1,6,1,512]{3,2,1,0:T(1,128)S(1)} %get-tuple-element.15), channel_id=1, source_target_pairs={{2,0},{3,1},{6,4},{7,5},{10,8},{11,9},{14,12},{15,13},{18,16},{19,... | collective-permute-start | bytes 36872 | tf_op jit(solution)/shard_map/ppermute | solution.py:19
  71.7 4.2 %collective-permute-done.6 = f32[1,6,1,512]{3,2,1,0:T(1,128)S(1)} collective-permute-done((f32[1,6,1,512]{3,2,1,0:T(1,128)S(1)}, f32[1,6,1,512]{3,2,1,0:T(1,128)S(1)}, u32[]{:S(2)}, u32[]{:S(2)}) %collective-permute-start.6) | collective-permute-done | bytes 12320 | tf_op jit(solution)/shard_map/ppermute | solution.py:19
  76.7 3.4 %fusion.37 = f32[1,4,128,512]{3,2,1,0:T(8,128)S(1)} fusion(f32[1,4,128,512]{3,2,1,0:T(8,128)S(1)} %fusion.11, f32[1,6,130,514]{3,2,1,0:T(8,128)S(1)} %select_maximum_fusion, f32[1,6,1,512]{3,2,1,0:T(1,128)S(1)} %collective-permute-done.7, f32[1,1,128,512]{3,2,1,0:T(8,128)S(1)} %collective-permute-done.4, f32[1,1,128,512]{3,2,1,0:T(8,128)S(1)} %collective-permute-done.5, ...), kind=kLoop, calls=%fused_computation.73 | loop fusion | flops 11010048 | bytes 12705792 | tf_op jit(solution)/shard_map/add | solution.py:49
  80.2 3.6 %collective-permute-start.9 = (f32[2,1,128,512]{3,2,1,0:T(8,128)S(1)}, f32[2,1,128,512]{3,2,1,0:T(8,128)S(1)}, u32[]{:S(2)}, u32[]{:S(2)}) collective-permute-start(f32[2,1,128,512]{3,2,1,0:T(8,128)S(1)} %get-tuple-element.10), channel_id=1, source_target_pairs={{0,4},{4,8},{8,12},{1,5},{5,9},{9,13},{2,6},{6,10},{10,14},{3,7},{... | collective-permute-start | bytes 1572872 | tf_op jit(solution)/shard_map/ppermute | solution.py:17
  83.8 1.3 %collective-permute-start.8 = (f32[2,1,128,512]{3,2,1,0:T(8,128)S(1)}, f32[2,1,128,512]{3,2,1,0:T(8,128)S(1)}, u32[]{:S(2)}, u32[]{:S(2)}) collective-permute-start(f32[2,1,128,512]{3,2,1,0:T(8,128)S(1)} %get-tuple-element.11), channel_id=1, source_target_pairs={{4,0},{8,4},{12,8},{5,1},{9,5},{13,9},{6,2},{10,6},{14,10},{7,3},{... | collective-permute-start | bytes 1572872 | tf_op jit(solution)/shard_map/ppermute | solution.py:19
  85.1 5.3 %collective-permute-done.9 = f32[2,1,128,512]{3,2,1,0:T(8,128)S(1)} collective-permute-done((f32[2,1,128,512]{3,2,1,0:T(8,128)S(1)}, f32[2,1,128,512]{3,2,1,0:T(8,128)S(1)}, u32[]{:S(2)}, u32[]{:S(2)}) %collective-permute-start.9) | collective-permute-done | bytes 524320 | tf_op jit(solution)/shard_map/ppermute | solution.py:17
  90.4 4.4 %collective-permute-done.8 = f32[2,1,128,512]{3,2,1,0:T(8,128)S(1)} collective-permute-done((f32[2,1,128,512]{3,2,1,0:T(8,128)S(1)}, f32[2,1,128,512]{3,2,1,0:T(8,128)S(1)}, u32[]{:S(2)}, u32[]{:S(2)}) %collective-permute-start.8) | collective-permute-done | bytes 524320 | tf_op jit(solution)/shard_map/ppermute | solution.py:19
  94.9 1.6 %collective-permute-start.11 = (f32[2,6,1,512]{3,2,1,0:T(1,128)S(1)}, f32[2,6,1,512]{3,2,1,0:T(1,128)S(1)}, u32[]{:S(2)}, u32[]{:S(2)}) collective-permute-start(f32[2,6,1,512]{3,2,1,0:T(1,128)S(1)} %get-tuple-element.6), channel_id=1, source_target_pairs={{0,2},{1,3},{4,6},{5,7},{8,10},{9,11},{12,14},{13,15},{16,18},{17,... | collective-permute-start | bytes 73736 | tf_op jit(solution)/shard_map/ppermute | solution.py:17
  96.6 1.3 %collective-permute-start.10 = (f32[2,6,1,512]{3,2,1,0:T(1,128)S(1)}, f32[2,6,1,512]{3,2,1,0:T(1,128)S(1)}, u32[]{:S(2)}, u32[]{:S(2)}) collective-permute-start(f32[2,6,1,512]{3,2,1,0:T(1,128)S(1)} %get-tuple-element.7), channel_id=1, source_target_pairs={{2,0},{3,1},{6,4},{7,5},{10,8},{11,9},{14,12},{15,13},{18,16},{19,... | collective-permute-start | bytes 73736 | tf_op jit(solution)/shard_map/ppermute | solution.py:19
  98.1 4.2 %collective-permute-done.10 = f32[2,6,1,512]{3,2,1,0:T(1,128)S(1)} collective-permute-done((f32[2,6,1,512]{3,2,1,0:T(1,128)S(1)}, f32[2,6,1,512]{3,2,1,0:T(1,128)S(1)}, u32[]{:S(2)}, u32[]{:S(2)}) %collective-permute-start.10) | collective-permute-done | bytes 24608 | tf_op jit(solution)/shard_map/ppermute | solution.py:19
  103.1 4.4 %fusion.17 = f32[1,4,128,512]{3,2,1,0:T(8,128)} fusion(f32[1,4,128,512]{3,2,1,0:T(8,128)S(1)} %copy-done.1, f32[1,6,130,512]{3,2,1,0:T(8,128)S(1)} %get-tuple-element.3, f32[1,4,128,512]{3,2,1,0:T(8,128)S(1)} %fusion.37, f32[1,6,130,512]{3,2,1,0:T(8,128)S(1)} %get-tuple-element.2, f32[2,6,1,512]{3,2,1,0:T(1,128)S(1)} %collective-permute-done.11, ...), kind=kLoop, calls=%fused_computation.36 | loop fusion | flops 12582912 | bytes 7438336 | tf_op jit(solution)/shard_map/mul | solution.py:59
  107.5 7.9 %all-gather.2.cloned.1.call-done = f32[2,4,128,512]{3,2,1,0:T(8,128)} async-done(((f32[1,4,128,512]{3,2,1,0:T(8,128)}), f32[2,4,128,512]{3,2,1,0:T(8,128)}) %all-gather.2.cloned.1.call-update) | async-done | bytes 2097168 | tf_op jit(solution)/shard_map/all_gather | solution.py:95
  115.4 2.9 %reduce_sum.8 = f32[4,128,512]{2,1,0:T(8,128)} reduce(f32[2,4,128,512]{3,2,1,0:T(8,128)} %all-gather.2.cloned.1.call-done, f32[]{:T(128)} %constant.13.clone.1), dimensions={0}, to_apply=%region_1.2 | reduce | flops 262144 | bytes 3145732 | tf_op jit(solution)/shard_map/reduce_sum | solution.py:95
  (32 shorter events, 2.5 us)
Async XLA Ops:
  7.2 23.9 %copy-start.2 = (f32[1,4,128,512]{3,2,1,0:T(8,128)S(1)}, f32[1,4,128,512]{3,2,1,0:T(8,128)}, u32[]{:S(2)}) copy-start(f32[1,4,128,512]{3,2,1,0:T(8,128)} %param.9) | copy-start | bytes 3145732
  7.2 23.9 %copy-start.3 = (f32[4,128,512]{2,1,0:T(8,128)S(1)}, f32[4,128,512]{2,1,0:T(8,128)}, u32[]{:S(2)}) copy-start(f32[4,128,512]{2,1,0:T(8,128)} %param.5) | copy-start | bytes 3145732
  7.2 9.6 %copy-start.5 = (s32[1,3,64]{2,0,1:T(1,128)S(1)}, s32[1,3,64]{2,0,1:T(1,128)}, u32[]{:S(2)}) copy-start(s32[1,3,64]{2,0,1:T(1,128)} %param.6) | copy-start | bytes 2308
  7.2 9.7 %copy-start.1 = (f32[1,4,128,512]{3,2,1,0:T(8,128)S(1)}, f32[1,4,128,512]{3,2,1,0:T(8,128)}, u32[]{:S(2)}) copy-start(f32[1,4,128,512]{3,2,1,0:T(8,128)} %param.8) | copy-start | bytes 3145732
  7.2 108.2 %all-gather.2.cloned.1.call-start = ((), (), s32[]{:S(2)}) async-start(), calls=%async_computation | async-start | bytes 3145728 | tf_op jit(solution)/shard_map/all_gather | solution.py:95
  9.6 27.0 %copy-start.6 = (f32[1,64]{1,0:T(1,128)S(1)}, f32[1,64]{1,0:T(1,128)}, u32[]{:S(2)}) copy-start(f32[1,64]{1,0:T(1,128)} %param.7) | copy-start | bytes 772
  9.6 16.6 %collective-permute-start = (f32[2,1,128,512]{3,2,1,0:T(8,128)}, f32[2,1,128,512]{3,2,1,0:T(8,128)}, u32[]{:S(2)}, u32[]{:S(2)}) collective-permute-start(f32[2,1,128,512]{3,2,1,0:T(8,128)} %get-tuple-element.12), channel_id=1, source_target_pairs={{0,4},{4,8},{8,12},{1,5},{5,9},{9,13},{2,6},{6,10},{10,14},{3,7},{... | collective-permute-start | bytes 1572872 | tf_op jit(solution)/shard_map/ppermute | solution.py:17
  15.5 15.6 %collective-permute-start.1 = (f32[2,1,128,512]{3,2,1,0:T(8,128)}, f32[2,1,128,512]{3,2,1,0:T(8,128)}, u32[]{:S(2)}, u32[]{:S(2)}) collective-permute-start(f32[2,1,128,512]{3,2,1,0:T(8,128)} %get-tuple-element.13), channel_id=1, source_target_pairs={{4,0},{8,4},{12,8},{5,1},{9,5},{13,9},{6,2},{10,6},{14,10},{7,3},{... | collective-permute-start | bytes 1572872 | tf_op jit(solution)/shard_map/ppermute | solution.py:19
  32.0 15.2 %collective-permute-start.2 = (f32[2,6,1,512]{3,2,1,0:T(1,128)S(1)}, f32[2,6,1,512]{3,2,1,0:T(1,128)S(1)}, u32[]{:S(2)}, u32[]{:S(2)}) collective-permute-start(f32[2,6,1,512]{3,2,1,0:T(1,128)S(1)} %get-tuple-element.8), channel_id=1, source_target_pairs={{0,2},{1,3},{4,6},{5,7},{8,10},{9,11},{12,14},{13,15},{16,18},{17,... | collective-permute-start | bytes 73736 | tf_op jit(solution)/shard_map/ppermute | solution.py:17
  35.4 11.8 %collective-permute-start.3 = (f32[2,6,1,512]{3,2,1,0:T(1,128)S(1)}, f32[2,6,1,512]{3,2,1,0:T(1,128)S(1)}, u32[]{:S(2)}, u32[]{:S(2)}) collective-permute-start(f32[2,6,1,512]{3,2,1,0:T(1,128)S(1)} %get-tuple-element.9), channel_id=1, source_target_pairs={{2,0},{3,1},{6,4},{7,5},{10,8},{11,9},{14,12},{15,13},{18,16},{19,... | collective-permute-start | bytes 73736 | tf_op jit(solution)/shard_map/ppermute | solution.py:19
  48.8 1.2 copy-start.4
  54.8 6.8 %collective-permute-start.5 = (f32[1,1,128,512]{3,2,1,0:T(8,128)S(1)}, f32[1,1,128,512]{3,2,1,0:T(8,128)S(1)}, u32[]{:S(2)}, u32[]{:S(2)}) collective-permute-start(f32[1,1,128,512]{3,2,1,0:T(8,128)S(1)} %get-tuple-element.16), channel_id=1, source_target_pairs={{0,4},{4,8},{8,12},{1,5},{5,9},{9,13},{2,6},{6,10},{10,14},{3,7},{... | collective-permute-start | bytes 786440 | tf_op jit(solution)/shard_map/ppermute | solution.py:17
  57.5 8.3 %collective-permute-start.4 = (f32[1,1,128,512]{3,2,1,0:T(8,128)S(1)}, f32[1,1,128,512]{3,2,1,0:T(8,128)S(1)}, u32[]{:S(2)}, u32[]{:S(2)}) collective-permute-start(f32[1,1,128,512]{3,2,1,0:T(8,128)S(1)} %get-tuple-element.17), channel_id=1, source_target_pairs={{4,0},{8,4},{12,8},{5,1},{9,5},{13,9},{6,2},{10,6},{14,10},{7,3},{... | collective-permute-start | bytes 786440 | tf_op jit(solution)/shard_map/ppermute | solution.py:19
  65.8 6.0 %collective-permute-start.7 = (f32[1,6,1,512]{3,2,1,0:T(1,128)S(1)}, f32[1,6,1,512]{3,2,1,0:T(1,128)S(1)}, u32[]{:S(2)}, u32[]{:S(2)}) collective-permute-start(f32[1,6,1,512]{3,2,1,0:T(1,128)S(1)} %get-tuple-element.14), channel_id=1, source_target_pairs={{0,2},{1,3},{4,6},{5,7},{8,10},{9,11},{12,14},{13,15},{16,18},{17,... | collective-permute-start | bytes 36872 | tf_op jit(solution)/shard_map/ppermute | solution.py:17
  70.3 5.6 %collective-permute-start.6 = (f32[1,6,1,512]{3,2,1,0:T(1,128)S(1)}, f32[1,6,1,512]{3,2,1,0:T(1,128)S(1)}, u32[]{:S(2)}, u32[]{:S(2)}) collective-permute-start(f32[1,6,1,512]{3,2,1,0:T(1,128)S(1)} %get-tuple-element.15), channel_id=1, source_target_pairs={{2,0},{3,1},{6,4},{7,5},{10,8},{11,9},{14,12},{15,13},{18,16},{19,... | collective-permute-start | bytes 36872 | tf_op jit(solution)/shard_map/ppermute | solution.py:19
  80.1 23.0 %copy-start = (f32[1,4,128,512]{3,2,1,0:T(8,128)}, f32[1,4,128,512]{3,2,1,0:T(8,128)S(1)}, u32[]{:S(2)}) copy-start(f32[1,4,128,512]{3,2,1,0:T(8,128)S(1)} %fusion.37) | copy-start | bytes 3145732
  80.2 10.2 %collective-permute-start.9 = (f32[2,1,128,512]{3,2,1,0:T(8,128)S(1)}, f32[2,1,128,512]{3,2,1,0:T(8,128)S(1)}, u32[]{:S(2)}, u32[]{:S(2)}) collective-permute-start(f32[2,1,128,512]{3,2,1,0:T(8,128)S(1)} %get-tuple-element.10), channel_id=1, source_target_pairs={{0,4},{4,8},{8,12},{1,5},{5,9},{9,13},{2,6},{6,10},{10,14},{3,7},{... | collective-permute-start | bytes 1572872 | tf_op jit(solution)/shard_map/ppermute | solution.py:17
  83.8 11.1 %collective-permute-start.8 = (f32[2,1,128,512]{3,2,1,0:T(8,128)S(1)}, f32[2,1,128,512]{3,2,1,0:T(8,128)S(1)}, u32[]{:S(2)}, u32[]{:S(2)}) collective-permute-start(f32[2,1,128,512]{3,2,1,0:T(8,128)S(1)} %get-tuple-element.11), channel_id=1, source_target_pairs={{4,0},{8,4},{12,8},{5,1},{9,5},{13,9},{6,2},{10,6},{14,10},{7,3},{... | collective-permute-start | bytes 1572872 | tf_op jit(solution)/shard_map/ppermute | solution.py:19
  94.9 3.2 %collective-permute-start.11 = (f32[2,6,1,512]{3,2,1,0:T(1,128)S(1)}, f32[2,6,1,512]{3,2,1,0:T(1,128)S(1)}, u32[]{:S(2)}, u32[]{:S(2)}) collective-permute-start(f32[2,6,1,512]{3,2,1,0:T(1,128)S(1)} %get-tuple-element.6), channel_id=1, source_target_pairs={{0,2},{1,3},{4,6},{5,7},{8,10},{9,11},{12,14},{13,15},{16,18},{17,... | collective-permute-start | bytes 73736 | tf_op jit(solution)/shard_map/ppermute | solution.py:17
  96.6 5.7 %collective-permute-start.10 = (f32[2,6,1,512]{3,2,1,0:T(1,128)S(1)}, f32[2,6,1,512]{3,2,1,0:T(1,128)S(1)}, u32[]{:S(2)}, u32[]{:S(2)}) collective-permute-start(f32[2,6,1,512]{3,2,1,0:T(1,128)S(1)} %get-tuple-element.7), channel_id=1, source_target_pairs={{2,0},{3,1},{6,4},{7,5},{10,8},{11,9},{14,12},{15,13},{18,16},{19,... | collective-permute-start | bytes 73736 | tf_op jit(solution)/shard_map/ppermute | solution.py:19
Sparse Core Ops, SparseCore 0:
  107.6 7.7 all-gather.1
